TPU v7x, 128 devices: a whole 4x4x4 slice. The times are simulated.
128 devices in a mesh: body: 2 (over y_lo), row: 8 (over y_hi, x), col: 8 (over z, core).
Axes of the slice: x: 4, y: 4 (y_hi: 2, y_lo: 2; y = y_hi * 2 + y_lo), z: 4, core: 2. Of those that a mesh axis runs over, the one named last changes fastest.
Arguments:
- lam_start: float32 [2, 128, 16384], P('body', None, ('row', 'col')), may hold values from -8 to 8
- load: float32 [2, 128, 16384], P('body', None, ('row', 'col')), may hold values from -24 to 24
- operator: bfloat16 [2, 16384, 8, 8, 256], P('body', 'row', None, 'col'), as said below
- partner: int32 [2, 16384], P('body', ('row', 'col')), may hold values from 0 to 16383, as said below
- active: int32 [16384], P(('row', 'col')), may hold values 0 or 1
- bounds: int32 [2, 2], P('body'), may hold values from 1 to 20, as said below
Outputs:
- multipliers: float32 [2, 128, 16384], P('body', None, ('row', 'col'))
- residual: float32 [2, 128, 16384], P('body', None, ('row', 'col'))
Inputs may be any that keep to these rules, and one draw needn't show every extreme that they name: Each operator F_b is symmetric, with positive diagonal. partner[0] maps every aligned block of 256 unknowns onto itself, one to one, and partner[1] is its inverse: partner[1, partner[0, i]] = i. bounds[b, 0] is 1 or 2 and bounds[b, 1] is 18 to 20.
All inputs are finite; a program needn't handle non-finite values. No bound on the sum of `active` on one device may be relied on, other than what follows from the above.
Results may differ from a plain program's by a relative error of at most 0.03.
The roundings to bfloat16 on the way count: a program that leaves them out, or rounds other values in their place, can miss the bound.
Values may be sent and summed in bfloat16 or wider, within the bound.
No kernel may reach another device: no remote copies, remote signals or barrier semaphores. Data moves between devices by JAX's collectives and lax.ppermute only.
A program may use at most 64 MiB of HBM per device.

v0:
```python
import jax
import jax.numpy as jnp
from jax import lax
from jax.sharding import PartitionSpec as P

K = 4


def swapped(value, axis, distance):
    mask = 2**distance
    pairs = [(source, source ^ mask) for source in range(lax.axis_size(axis))]
    return lax.ppermute(value, axis, pairs)


def clamp_local(lam, partner, active):
    peer = swapped(lam, "body", 0)
    width = lam.shape[1]
    local = partner % width
    mate = jnp.take(peer, local, axis=1)
    which = lax.axis_index("body")
    sign = (1 - 2 * which).astype(jnp.float32)
    flag_index = jnp.where(which == 0, jnp.arange(width, dtype=jnp.int32), local)
    flags = jnp.take(active, flag_index) > 0
    middle = 0.5 * (lam + mate)
    normal = 0.5 * sign * (lam - mate)
    normal = jnp.where(flags[None, :], jnp.maximum(normal, 0.0), normal)
    return middle + sign * normal


def apply_tile(field, tile):
    rounded = field.astype(jnp.bfloat16)
    partial_sum = lax.dot_general(
        lax.all_gather(rounded, "row", axis=1, tiled=True),
        tile,
        (((1,), (1,)), ((), ())),
        preferred_element_type=jnp.float32,
    )
    return lax.psum_scatter(partial_sum, "col", scatter_dimension=1, tiled=True)


def cheb_local(start, load, tile, lower, upper):
    theta = 0.5 * (upper + lower)
    delta = 0.5 * (upper - lower)
    sigma = theta / delta
    answer = start
    resid = load - apply_tile(answer, tile)
    direction = resid / theta
    rho = delta / theta
    for step in range(K):
        answer = answer + direction
        resid = resid - apply_tile(direction, tile)
        if step + 1 < K:
            rho_new = 1.0 / (2.0 * sigma - rho)
            direction = rho_new * rho * direction + 2.0 * rho_new / delta * resid
            rho = rho_new
    return (answer, resid)


def per_device(lam_start, load, operator, partner, active, bounds):
    tile = operator.reshape(operator.shape[1], operator.shape[2] * operator.shape[4])
    lower = bounds[0, 0].astype(jnp.float32)
    upper = bounds[0, 1].astype(jnp.float32)
    own_load = load[0]
    own_partner = partner[0]
    first = clamp_local(lam_start[0], own_partner, active)
    second, unused = cheb_local(first, own_load, tile, lower, upper)
    third = clamp_local(second, own_partner, active)
    answer, resid = cheb_local(third, own_load, tile, lower, upper)
    return (answer[None], resid[None])


def solution(mesh):
    return jax.shard_map(
        per_device,
        mesh=mesh,
        in_specs=(
            P("body", None, ("row", "col")),
            P("body", None, ("row", "col")),
            P("body", "row", None, "col", None),
            P("body", ("row", "col")),
            P(("row", "col")),
            P("body", None),
        ),
        out_specs=(P("body", None, ("row", "col")), P("body", None, ("row", "col"))),
        check_vma=False,
    )
```

profile of v0, /device:TPU:0, one launch (start us, length us, event | category | flops | bytes accessed | tf_op | source)
XLA Modules:
  0.0 709.3 jit_solution(16832281575850132127)
XLA Ops:
  7.2 0.0 reduce-scatter.10.cloned.1.call-start
  7.2 1.8 collective-permute-start
  9.0 0.7 compare_and_fusion
  9.7 1.9 gather_fusion.1
  11.7 10.3 %copy.16 = bf16[256,8,8,256]{3,1,2,0:T(8,128)(2,1)} copy(bf16[256,8,8,256]{3,2,1,0:T(8,128)(2,1)} %bitcast.89) | data formatting | bytes 16777216
  22.1 0.1 copy.12
  22.2 0.7 gather_fusion
  22.9 0.1 copy.13
  23.0 0.1 fusion.17
  23.1 35.3 %all_gather.27 = bf16[128,2048]{1,0:T(8,128)(2,1)S(1)} all-gather(bf16[128,256]{1,0:T(8,128)(2,1)S(1)} %fusion.17), channel_id=1, replica_groups=mesh['body'=2,'row'=8,'col'=8] {'row'}, dimensions={1}, use_global_device_ids=true | all-gather | bytes 589824 | tf_op jit(solution)/shard_map/all_gather | solution.py:33
  58.4 7.3 %fusion.24 = f32[128,2048]{1,0:T(8,128)} fusion(bf16[128,2048]{1,0:T(8,128)(2,1)S(1)} %all_gather.27, bf16[2048,2048]{1,0:T(8,128)(2,1)} %bitcast.80), kind=kOutput, calls=%fused_computation.52 | convolution fusion | flops 1073741824 | bytes 9961472 | tf_op jit(solution)/shard_map/dot_general | solution.py:32
  65.7 0.0 reduce-scatter.10.cloned.1.call-update
  65.7 0.0 reduce-scatter.12.cloned.1.call-start
  65.8 0.6 fusion.23
  67.7 32.2 %reduce-scatter.10.cloned.1.call-done = f32[128,256]{1,0:T(8,128)} async-done(((f32[128,2048]{1,0:T(8,128)}), f32[128,256]{1,0:T(8,128)}) %reduce-scatter.10.cloned.1.call-update) | async-done | bytes 131088 | tf_op jit(solution)/shard_map/reduce_scatter | solution.py:38
  99.9 1.0 fusion.22
  100.9 35.5 %all_gather.28 = bf16[128,2048]{1,0:T(8,128)(2,1)S(1)} all-gather(bf16[128,256]{1,0:T(8,128)(2,1)S(1)} %get-tuple-element.17), channel_id=1, replica_groups=mesh['body'=2,'row'=8,'col'=8] {'row'}, dimensions={1}, use_global_device_ids=true | all-gather | bytes 589824 | tf_op jit(solution)/shard_map/all_gather | solution.py:33
  136.3 7.4 %fusion.25 = f32[128,2048]{1,0:T(8,128)} fusion(bf16[128,2048]{1,0:T(8,128)(2,1)S(1)} %all_gather.28, bf16[2048,2048]{1,0:T(8,128)(2,1)} %bitcast.81), kind=kOutput, calls=%fused_computation.53 | convolution fusion | flops 1073741824 | bytes 9961472 | tf_op jit(solution)/shard_map/dot_general | solution.py:32
  143.7 0.0 reduce-scatter.14.cloned.1.call-start
  143.9 30.1 %reduce-scatter.12.cloned.1.call-done = f32[128,256]{1,0:T(8,128)} async-done(((f32[128,2048]{1,0:T(8,128)}), f32[128,256]{1,0:T(8,128)}) %reduce-scatter.12.cloned.1.call-update) | async-done | bytes 131088 | tf_op jit(solution)/shard_map/reduce_scatter | solution.py:38
  174.1 1.0 fusion.12
  175.0 35.7 %all_gather.29 = bf16[128,2048]{1,0:T(8,128)(2,1)S(1)} all-gather(bf16[128,256]{1,0:T(8,128)(2,1)S(1)} %get-tuple-element.15), channel_id=1, replica_groups=mesh['body'=2,'row'=8,'col'=8] {'row'}, dimensions={1}, use_global_device_ids=true | all-gather | bytes 589824 | tf_op jit(solution)/shard_map/all_gather | solution.py:33
  210.7 7.3 %fusion.26 = f32[128,2048]{1,0:T(8,128)} fusion(bf16[128,2048]{1,0:T(8,128)(2,1)S(1)} %all_gather.29, bf16[2048,2048]{1,0:T(8,128)(2,1)} %bitcast.82), kind=kOutput, calls=%fused_computation.54 | convolution fusion | flops 1073741824 | bytes 9961472 | tf_op jit(solution)/shard_map/dot_general | solution.py:32
  218.1 0.0 reduce-scatter.14.cloned.1.call-update
  218.1 0.0 reduce-scatter.16.cloned.1.call-start
  218.2 30.2 %reduce-scatter.14.cloned.1.call-done = f32[128,256]{1,0:T(8,128)} async-done(((f32[128,2048]{1,0:T(8,128)}), f32[128,256]{1,0:T(8,128)}) %reduce-scatter.14.cloned.1.call-update) | async-done | bytes 131088 | tf_op jit(solution)/shard_map/reduce_scatter | solution.py:38
  248.5 1.0 fusion.8
  249.4 35.5 %all_gather.30 = bf16[128,2048]{1,0:T(8,128)(2,1)S(1)} all-gather(bf16[128,256]{1,0:T(8,128)(2,1)S(1)} %get-tuple-element.13), channel_id=1, replica_groups=mesh['body'=2,'row'=8,'col'=8] {'row'}, dimensions={1}, use_global_device_ids=true | all-gather | bytes 589824 | tf_op jit(solution)/shard_map/all_gather | solution.py:33
  284.9 7.4 %fusion.27 = f32[128,2048]{1,0:T(8,128)} fusion(bf16[128,2048]{1,0:T(8,128)(2,1)S(1)} %all_gather.30, bf16[2048,2048]{1,0:T(8,128)(2,1)} %bitcast.83), kind=kOutput, calls=%fused_computation.55 | convolution fusion | flops 1073741824 | bytes 9961472 | tf_op jit(solution)/shard_map/dot_general | solution.py:32
  292.3 0.0 reduce-scatter.16.cloned.1.call-update
  292.3 0.0 reduce-scatter.18.cloned.1.call-start
  292.4 30.2 %reduce-scatter.16.cloned.1.call-done = f32[128,256]{1,0:T(8,128)} async-done(((f32[128,2048]{1,0:T(8,128)}), f32[128,256]{1,0:T(8,128)}) %reduce-scatter.16.cloned.1.call-update) | async-done | bytes 131088 | tf_op jit(solution)/shard_map/reduce_scatter | solution.py:38
  322.7 1.0 add_add_fusion
  323.7 1.6 collective-permute-start.1
  325.2 3.5 collective-permute-done.1
  328.7 0.1 copy.14
  328.8 0.7 gather_fusion.2
  329.6 0.1 copy.15
  329.7 0.1 fusion.16
  329.7 35.3 %all_gather.31 = bf16[128,2048]{1,0:T(8,128)(2,1)S(1)} all-gather(bf16[128,256]{1,0:T(8,128)(2,1)S(1)} %fusion.16), channel_id=1, replica_groups=mesh['body'=2,'row'=8,'col'=8] {'row'}, dimensions={1}, use_global_device_ids=true | all-gather | bytes 589824 | tf_op jit(solution)/shard_map/all_gather | solution.py:33
  365.1 7.3 %fusion.28 = f32[128,2048]{1,0:T(8,128)} fusion(bf16[128,2048]{1,0:T(8,128)(2,1)S(1)} %all_gather.31, bf16[2048,2048]{1,0:T(8,128)(2,1)} %bitcast.84), kind=kOutput, calls=%fused_computation.56 | convolution fusion | flops 1073741824 | bytes 9961472 | tf_op jit(solution)/shard_map/dot_general | solution.py:32
  372.4 0.0 reduce-scatter.18.cloned.1.call-update
  372.4 0.0 reduce-scatter.20.cloned.1.call-start
  372.5 31.1 %reduce-scatter.18.cloned.1.call-done = f32[128,256]{1,0:T(8,128)} async-done(((f32[128,2048]{1,0:T(8,128)}), f32[128,256]{1,0:T(8,128)}) %reduce-scatter.18.cloned.1.call-update) | async-done | bytes 131088 | tf_op jit(solution)/shard_map/reduce_scatter | solution.py:38
  403.6 1.0 fusion.20
  404.6 35.5 %all_gather.32 = bf16[128,2048]{1,0:T(8,128)(2,1)S(1)} all-gather(bf16[128,256]{1,0:T(8,128)(2,1)S(1)} %get-tuple-element.11), channel_id=1, replica_groups=mesh['body'=2,'row'=8,'col'=8] {'row'}, dimensions={1}, use_global_device_ids=true | all-gather | bytes 589824 | tf_op jit(solution)/shard_map/all_gather | solution.py:33
  440.1 7.4 %fusion.29 = f32[128,2048]{1,0:T(8,128)} fusion(bf16[128,2048]{1,0:T(8,128)(2,1)S(1)} %all_gather.32, bf16[2048,2048]{1,0:T(8,128)(2,1)} %bitcast.85), kind=kOutput, calls=%fused_computation.57 | convolution fusion | flops 1073741824 | bytes 9961472 | tf_op jit(solution)/shard_map/dot_general | solution.py:32
  447.5 0.0 reduce-scatter.22.cloned.1.call-start
  447.5 30.3 %reduce-scatter.20.cloned.1.call-done = f32[128,256]{1,0:T(8,128)} async-done(((f32[128,2048]{1,0:T(8,128)}), f32[128,256]{1,0:T(8,128)}) %reduce-scatter.20.cloned.1.call-update) | async-done | bytes 131088 | tf_op jit(solution)/shard_map/reduce_scatter | solution.py:38
  477.9 1.0 fusion.13
  478.8 35.8 %all_gather.33 = bf16[128,2048]{1,0:T(8,128)(2,1)S(1)} all-gather(bf16[128,256]{1,0:T(8,128)(2,1)S(1)} %get-tuple-element.9), channel_id=1, replica_groups=mesh['body'=2,'row'=8,'col'=8] {'row'}, dimensions={1}, use_global_device_ids=true | all-gather | bytes 589824 | tf_op jit(solution)/shard_map/all_gather | solution.py:33
  514.6 7.4 %fusion.30 = f32[128,2048]{1,0:T(8,128)} fusion(bf16[128,2048]{1,0:T(8,128)(2,1)S(1)} %all_gather.33, bf16[2048,2048]{1,0:T(8,128)(2,1)} %bitcast.86), kind=kOutput, calls=%fused_computation.58 | convolution fusion | flops 1073741824 | bytes 9961472 | tf_op jit(solution)/shard_map/dot_general | solution.py:32
  522.0 0.0 reduce-scatter.24.cloned.1.call-start
  522.1 30.5 %reduce-scatter.22.cloned.1.call-done = f32[128,256]{1,0:T(8,128)} async-done(((f32[128,2048]{1,0:T(8,128)}), f32[128,256]{1,0:T(8,128)}) %reduce-scatter.22.cloned.1.call-update) | async-done | bytes 131088 | tf_op jit(solution)/shard_map/reduce_scatter | solution.py:38
  552.5 1.0 fusion.18
  553.5 35.5 %all_gather.34 = bf16[128,2048]{1,0:T(8,128)(2,1)S(1)} all-gather(bf16[128,256]{1,0:T(8,128)(2,1)S(1)} %get-tuple-element.6), channel_id=1, replica_groups=mesh['body'=2,'row'=8,'col'=8] {'row'}, dimensions={1}, use_global_device_ids=true | all-gather | bytes 589824 | tf_op jit(solution)/shard_map/all_gather | solution.py:33
  588.9 7.4 %fusion.31 = f32[128,2048]{1,0:T(8,128)} fusion(bf16[128,2048]{1,0:T(8,128)(2,1)S(1)} %all_gather.34, bf16[2048,2048]{1,0:T(8,128)(2,1)} %bitcast.87), kind=kOutput, calls=%fused_computation.59 | convolution fusion | flops 1073741824 | bytes 9961472 | tf_op jit(solution)/shard_map/dot_general | solution.py:32
  596.3 0.0 reduce-scatter.26.cloned.1.call-start
  596.4 30.5 %reduce-scatter.24.cloned.1.call-done = f32[128,256]{1,0:T(8,128)} async-done(((f32[128,2048]{1,0:T(8,128)}), f32[128,256]{1,0:T(8,128)}) %reduce-scatter.24.cloned.1.call-update) | async-done | bytes 131088 | tf_op jit(solution)/shard_map/reduce_scatter | solution.py:38
  626.9 0.9 fusion.9
  627.8 35.4 %all_gather.35 = bf16[128,2048]{1,0:T(8,128)(2,1)S(1)} all-gather(bf16[128,256]{1,0:T(8,128)(2,1)S(1)} %get-tuple-element.4), channel_id=1, replica_groups=mesh['body'=2,'row'=8,'col'=8] {'row'}, dimensions={1}, use_global_device_ids=true | all-gather | bytes 589824 | tf_op jit(solution)/shard_map/all_gather | solution.py:33
  663.2 7.4 %fusion.32 = f32[128,2048]{1,0:T(8,128)} fusion(bf16[128,2048]{1,0:T(8,128)(2,1)S(1)} %all_gather.35, bf16[2048,2048]{1,0:T(8,128)(2,1)} %bitcast.88), kind=kOutput, calls=%fused_computation.60 | convolution fusion | flops 1073741824 | bytes 9961472 | tf_op jit(solution)/shard_map/dot_general | solution.py:32
  670.6 30.5 %reduce-scatter.26.cloned.1.call-done = f32[128,256]{1,0:T(8,128)} async-done(((f32[128,2048]{1,0:T(8,128)}), f32[128,256]{1,0:T(8,128)}) %reduce-scatter.26.cloned.1.call-update) | async-done | bytes 131088 | tf_op jit(solution)/shard_map/reduce_scatter | solution.py:38
  701.1 1.7 subtract_bitcast_fusion
  (22 shorter events, 0.1 us)
Async XLA Ops:
  7.2 2.6 copy-start
  7.2 92.7 %reduce-scatter.10.cloned.1.call-start = ((), (), s32[]{:S(2)}) async-start(), calls=%async_computation.9 | async-start | bytes 1179648 | tf_op jit(solution)/shard_map/reduce_scatter | solution.py:38
  7.2 14.8 %collective-permute-start = (f32[128,256]{1,0:T(8,128)}, f32[128,256]{1,0:T(8,128)S(1)}, u32[]{:S(2)}, u32[]{:S(2)}) collective-permute-start(f32[128,256]{1,0:T(8,128)} %bitcast.90), channel_id=1, source_target_pairs={{0,64},{64,0},{1,65},{65,1},{2,66},{66,2},{3,67},{67,3},{4,68},{68... | collective-permute-start | bytes 393224 | tf_op jit(solution)/shard_map/ppermute | solution.py:12
  11.7 11.3 %copy-start.2 = (f32[1,128,256]{2,1,0:T(8,128)S(1)}, f32[1,128,256]{2,1,0:T(8,128)}, u32[]{:S(2)}) copy-start(f32[1,128,256]{2,1,0:T(8,128)} %param.10) | copy-start | bytes 393220
  22.0 43.7 %copy-start.5 = (s32[1,2]{1,0:T(1,128)S(1)}, s32[1,2]{1,0:T(1,128)}, u32[]{:S(2)}) copy-start(s32[1,2]{1,0:T(1,128)} %param.15) | copy-start | bytes 28
  22.0 77.8 %copy-start.1 = (f32[1,128,256]{2,1,0:T(8,128)S(1)}, f32[1,128,256]{2,1,0:T(8,128)}, u32[]{:S(2)}) copy-start(f32[1,128,256]{2,1,0:T(8,128)} %param.11) | copy-start | bytes 393220
  65.7 108.4 %reduce-scatter.12.cloned.1.call-start = ((), (), s32[]{:S(2)}) async-start(), calls=%async_computation.10 | async-start | bytes 1179648 | tf_op jit(solution)/shard_map/reduce_scatter | solution.py:38
  99.9 74.2 %copy-start.3 = (f32[128,256]{1,0:T(8,128)S(1)}, f32[128,256]{1,0:T(8,128)}, u32[]{:S(2)}) copy-start(f32[128,256]{1,0:T(8,128)} %reduce-scatter.10.cloned.1.call-done) | copy-start | bytes 393220
  143.7 104.7 %reduce-scatter.14.cloned.1.call-start = ((), (), s32[]{:S(2)}) async-start(), calls=%async_computation.11 | async-start | bytes 1179648 | tf_op jit(solution)/shard_map/reduce_scatter | solution.py:38
  218.1 104.6 %reduce-scatter.16.cloned.1.call-start = ((), (), s32[]{:S(2)}) async-start(), calls=%async_computation.12 | async-start | bytes 1179648 | tf_op jit(solution)/shard_map/reduce_scatter | solution.py:38
  292.3 111.3 %reduce-scatter.18.cloned.1.call-start = ((), (), s32[]{:S(2)}) async-start(), calls=%async_computation.13 | async-start | bytes 1179648 | tf_op jit(solution)/shard_map/reduce_scatter | solution.py:38
  323.7 5.0 collective-permute-start.1
  372.4 105.5 %reduce-scatter.20.cloned.1.call-start = ((), (), s32[]{:S(2)}) async-start(), calls=%async_computation.14 | async-start | bytes 1179648 | tf_op jit(solution)/shard_map/reduce_scatter | solution.py:38
  403.6 74.3 %copy-start.4 = (f32[128,256]{1,0:T(8,128)S(1)}, f32[128,256]{1,0:T(8,128)}, u32[]{:S(2)}) copy-start(f32[128,256]{1,0:T(8,128)} %reduce-scatter.18.cloned.1.call-done) | copy-start | bytes 393220
  447.5 105.0 %reduce-scatter.22.cloned.1.call-start = ((), (), s32[]{:S(2)}) async-start(), calls=%async_computation.15 | async-start | bytes 1179648 | tf_op jit(solution)/shard_map/reduce_scatter | solution.py:38
  522.0 104.9 %reduce-scatter.24.cloned.1.call-start = ((), (), s32[]{:S(2)}) async-start(), calls=%async_computation.16 | async-start | bytes 1179648 | tf_op jit(solution)/shard_map/reduce_scatter | solution.py:38
  596.3 104.8 %reduce-scatter.26.cloned.1.call-start = ((), (), s32[]{:S(2)}) async-start(), calls=%async_computation.17 | async-start | bytes 1179648 | tf_op jit(solution)/shard_map/reduce_scatter | solution.py:38
Sparse Core Ops, SparseCore 0:
  65.9 33.9 reduce-scatter.9
  143.8 30.2 reduce-scatter.11
  218.2 30.2 reduce-scatter.13
  292.4 30.2 reduce-scatter.15
  372.6 31.0 reduce-scatter.17
  447.6 30.2 reduce-scatter.19
  522.1 30.3 reduce-scatter.21
  596.4 30.3 reduce-scatter.23
  670.7 30.3 reduce-scatter.25
where the time goes:
time: 710 us; the launch traced here: 709 us
  blocking collectives  319 us (45%)
  waiting for transfers between devices  279 us (39%)
  matrix products  66.2 us (9%)
  between operations  15.7 us (2%)
  local copies, waits for them, and re-layouts  14.7 us (2%)
  other arithmetic  10.3 us (1%)
    all_gather x9, blocking collectives, apply_tile(): lax.all_gather(rounded, 'row', axis=1, tiled=True)  319 us
    reduce_scatter x9, waiting for transfers between devices, apply_tile(): return lax.psum_scatter(partial_sum, 'col', scatter_dimension=1, tiled=True)  276 us
    dot_general x9, matrix products, apply_tile(): lax.dot_general(lax.all_gather(rounded, 'row', axis=1, tiled=True), tile,...  66.2 us
  transfers between devices with their start and end apart: 11, of which 10 were waited for; matrix products, arithmetic and copies ran while one was open for 2% of the time, Pallas kernels for 0%

commit v1 on v0

--- a/solution.py
+++ b/solution.py
@@ -4,6 +4,11 @@
 from jax.sharding import PartitionSpec as P
 
 K = 4
+
+
+def swapped_in(block, mesh_axis, along):
+    sent = jnp.stack([block] * lax.axis_size(mesh_axis))
+    return jnp.concatenate(lax.all_to_all(sent, mesh_axis, 0, 0), axis=along)
 
 
 def swapped(value, axis, distance):
@@ -30,7 +35,7 @@
 def apply_tile(field, tile):
     rounded = field.astype(jnp.bfloat16)
     partial_sum = lax.dot_general(
-        lax.all_gather(rounded, "row", axis=1, tiled=True),
+        swapped_in(rounded, "row", 1),
         tile,
         (((1,), (1,)), ((), ())),
         preferred_element_type=jnp.float32,

time: 710 us -> 526 us (0.74)
  blocking collectives: 319 us -> 134 us
  waiting for transfers between devices: 279 us -> 269 us
    all_gather x9 -> x0, blocking collectives: 319 us -> none  [apply_tile(): lax.all_gather(rounded, 'row', axis=1, tiled=True)]
    all_to_all x0 -> x8, blocking collectives: none -> 134 us  [swapped_in(): return jnp.concatenate(lax.all_to_all(sent, mesh_axis, 0, 0), axis=along)]
    reduce_scatter x9, waiting for transfers between devices: 276 us -> 264 us  [apply_tile(): return lax.psum_scatter(partial_sum, 'col', scatter_dimension=1, tiled=True)]
  transfers between devices with their start and end apart: 11 -> 12, of which waited for: 10 -> 12; matrix products, arithmetic and copies ran while one was open for 2% -> 3% of each run, Pallas kernels for 0% -> 0%
where the time goes in v1:
time: 526 us; the launch traced here: 524 us
  waiting for transfers between devices  269 us (51%)
  blocking collectives  134 us (25%)
  matrix products  66.6 us (13%)
  local copies, waits for them, and re-layouts  17.2 us (3%)
  between operations  15.8 us (3%)
  other arithmetic  11.2 us (2%)
  starting transfers between devices  10.7 us (2%)
    reduce_scatter x9, waiting for transfers between devices, apply_tile(): return lax.psum_scatter(partial_sum, 'col', scatter_dimension=1, tiled=True)  264 us
    all_to_all x8, blocking collectives, swapped_in(): return jnp.concatenate(lax.all_to_all(sent, mesh_axis, 0, 0), axis=along)  134 us
    dot_general x9, matrix products, apply_tile(): lax.dot_general(swapped_in(rounded, 'row', 1), tile, (((1,), (1,)), ((),...  66.6 us
  transfers between devices with their start and end apart: 12, of which 12 were waited for; matrix products, arithmetic and copies ran while one was open for 3% of the time, Pallas kernels for 0%

profile of v1, /device:TPU:0, one launch (start us, length us, event | category | flops | bytes accessed | tf_op | source)
XLA Modules:
  0.0 524.5 jit_solution(518387025785355464)
XLA Ops:
  7.2 1.8 collective-permute-start
  8.9 0.7 compare_and_fusion
  9.7 1.9 gather_fusion.1
  11.7 1.0 collective-permute-done
  12.7 0.1 copy.12
  12.8 0.7 gather_fusion
  13.5 0.1 copy.13
  13.6 1.0 fusion.17
  14.6 0.1 copy.14
  14.7 0.9 stack.18
  15.6 7.1 %all-to-all-start = ((bf16[8,128,256]{1,2,0:T(8,128)(2,1)}), bf16[8,128,256]{1,2,0:T(8,128)(2,1)S(1)}, u32[]{:S(2)}, u32[]{:S(2)}) async-start(bf16[8,128,256]{1,2,0:T(8,128)(2,1)} %stack.18), calls=%async_computation | async-start | bytes 1048576 | tf_op jit(solution)/shard_map/all_to_all | solution.py:11
  22.7 10.3 %copy.25 = bf16[256,8,8,256]{3,1,2,0:T(8,128)(2,1)} copy(bf16[256,8,8,256]{3,2,1,0:T(8,128)(2,1)} %bitcast.116) | data formatting | bytes 16777216
  33.0 0.4 all-to-all-done
  33.4 7.4 %fusion.24 = f32[128,2048]{1,0:T(8,128)} fusion(bf16[128,2048]{0,1:T(8,128)(2,1)S(1)} %bitcast.117, bf16[2048,2048]{1,0:T(8,128)(2,1)} %bitcast.107), kind=kOutput, calls=%fused_computation.52 | convolution fusion | flops 1073741824 | bytes 9961472 | tf_op jit(solution)/shard_map/dot_general | solution.py:37
  40.9 0.6 fusion.23
  42.8 32.9 %reduce-scatter.10.cloned.1.call-done = f32[128,256]{1,0:T(8,128)} async-done(((f32[128,2048]{1,0:T(8,128)}), f32[128,256]{1,0:T(8,128)}) %reduce-scatter.10.cloned.1.call-update) | async-done | bytes 131088 | tf_op jit(solution)/shard_map/reduce_scatter | solution.py:43
  75.7 1.0 fusion.22
  76.7 0.1 copy.15
  76.8 0.1 stack.19
  76.9 16.8 %all_to_all.45 = bf16[8,128,256]{1,2,0:T(8,128)(2,1)S(1)} all-to-all(bf16[8,128,256]{1,2,0:T(8,128)(2,1)S(1)} %stack.19), channel_id=1, replica_groups=mesh['body'=2,'row'=8,'col'=8] {'row'}, dimensions={0} | all-to-all | bytes 1048576 | tf_op jit(solution)/shard_map/all_to_all | solution.py:11
  93.7 7.4 %fusion.25 = f32[128,2048]{1,0:T(8,128)} fusion(bf16[128,2048]{0,1:T(8,128)(2,1)S(1)} %bitcast.119, bf16[2048,2048]{1,0:T(8,128)(2,1)} %bitcast.108), kind=kOutput, calls=%fused_computation.53 | convolution fusion | flops 1073741824 | bytes 9961472 | tf_op jit(solution)/shard_map/dot_general | solution.py:37
  101.3 28.7 %reduce-scatter.12.cloned.1.call-done = f32[128,256]{1,0:T(8,128)} async-done(((f32[128,2048]{1,0:T(8,128)}), f32[128,256]{1,0:T(8,128)}) %reduce-scatter.12.cloned.1.call-update) | async-done | bytes 131088 | tf_op jit(solution)/shard_map/reduce_scatter | solution.py:43
  130.0 1.0 fusion.12
  131.0 0.1 copy.16
  131.1 16.8 %all_to_all.46 = bf16[8,128,256]{1,2,0:T(8,128)(2,1)S(1)} all-to-all(bf16[8,128,256]{1,2,0:T(8,128)(2,1)S(1)} %stack.20), channel_id=1, replica_groups=mesh['body'=2,'row'=8,'col'=8] {'row'}, dimensions={0} | all-to-all | bytes 1048576 | tf_op jit(solution)/shard_map/all_to_all | solution.py:11
  147.9 7.4 %fusion.26 = f32[128,2048]{1,0:T(8,128)} fusion(bf16[128,2048]{0,1:T(8,128)(2,1)S(1)} %bitcast.120, bf16[2048,2048]{1,0:T(8,128)(2,1)} %bitcast.109), kind=kOutput, calls=%fused_computation.54 | convolution fusion | flops 1073741824 | bytes 9961472 | tf_op jit(solution)/shard_map/dot_general | solution.py:37
  155.5 28.8 %reduce-scatter.14.cloned.1.call-done = f32[128,256]{1,0:T(8,128)} async-done(((f32[128,2048]{1,0:T(8,128)}), f32[128,256]{1,0:T(8,128)}) %reduce-scatter.14.cloned.1.call-update) | async-done | bytes 131088 | tf_op jit(solution)/shard_map/reduce_scatter | solution.py:43
  184.3 1.0 fusion.8
  185.2 0.1 copy.17
  185.4 16.7 %all_to_all.47 = bf16[8,128,256]{1,2,0:T(8,128)(2,1)S(1)} all-to-all(bf16[8,128,256]{1,2,0:T(8,128)(2,1)S(1)} %stack.21), channel_id=1, replica_groups=mesh['body'=2,'row'=8,'col'=8] {'row'}, dimensions={0} | all-to-all | bytes 1048576 | tf_op jit(solution)/shard_map/all_to_all | solution.py:11
  202.1 7.4 %fusion.27 = f32[128,2048]{1,0:T(8,128)} fusion(bf16[128,2048]{0,1:T(8,128)(2,1)S(1)} %bitcast.121, bf16[2048,2048]{1,0:T(8,128)(2,1)} %bitcast.110), kind=kOutput, calls=%fused_computation.55 | convolution fusion | flops 1073741824 | bytes 9961472 | tf_op jit(solution)/shard_map/dot_general | solution.py:37
  209.7 28.8 %reduce-scatter.16.cloned.1.call-done = f32[128,256]{1,0:T(8,128)} async-done(((f32[128,2048]{1,0:T(8,128)}), f32[128,256]{1,0:T(8,128)}) %reduce-scatter.16.cloned.1.call-update) | async-done | bytes 131088 | tf_op jit(solution)/shard_map/reduce_scatter | solution.py:43
  238.5 1.0 add_add_fusion
  239.5 1.5 collective-permute-start.1
  241.0 3.6 collective-permute-done.1
  244.6 0.1 copy.18
  244.7 0.7 gather_fusion.2
  245.4 0.1 copy.19
  245.6 0.1 copy.20
  245.7 0.1 stack.22
  245.8 16.7 %all_to_all.48 = bf16[8,128,256]{1,2,0:T(8,128)(2,1)S(1)} all-to-all(bf16[8,128,256]{1,2,0:T(8,128)(2,1)S(1)} %stack.22), channel_id=1, replica_groups=mesh['body'=2,'row'=8,'col'=8] {'row'}, dimensions={0} | all-to-all | bytes 1048576 | tf_op jit(solution)/shard_map/all_to_all | solution.py:11
  262.5 7.4 %fusion.28 = f32[128,2048]{1,0:T(8,128)} fusion(bf16[128,2048]{0,1:T(8,128)(2,1)S(1)} %bitcast.122, bf16[2048,2048]{1,0:T(8,128)(2,1)} %bitcast.111), kind=kOutput, calls=%fused_computation.56 | convolution fusion | flops 1073741824 | bytes 9961472 | tf_op jit(solution)/shard_map/dot_general | solution.py:37
  270.0 29.4 %reduce-scatter.18.cloned.1.call-done = f32[128,256]{1,0:T(8,128)} async-done(((f32[128,2048]{1,0:T(8,128)}), f32[128,256]{1,0:T(8,128)}) %reduce-scatter.18.cloned.1.call-update) | async-done | bytes 131088 | tf_op jit(solution)/shard_map/reduce_scatter | solution.py:43
  299.3 1.0 fusion.20
  300.3 0.1 copy.21
  300.5 16.8 %all_to_all.49 = bf16[8,128,256]{1,2,0:T(8,128)(2,1)S(1)} all-to-all(bf16[8,128,256]{1,2,0:T(8,128)(2,1)S(1)} %stack.23), channel_id=1, replica_groups=mesh['body'=2,'row'=8,'col'=8] {'row'}, dimensions={0} | all-to-all | bytes 1048576 | tf_op jit(solution)/shard_map/all_to_all | solution.py:11
  317.3 7.4 %fusion.29 = f32[128,2048]{1,0:T(8,128)} fusion(bf16[128,2048]{0,1:T(8,128)(2,1)S(1)} %bitcast.123, bf16[2048,2048]{1,0:T(8,128)(2,1)} %bitcast.112), kind=kOutput, calls=%fused_computation.57 | convolution fusion | flops 1073741824 | bytes 9961472 | tf_op jit(solution)/shard_map/dot_general | solution.py:37
  324.8 28.9 %reduce-scatter.20.cloned.1.call-done = f32[128,256]{1,0:T(8,128)} async-done(((f32[128,2048]{1,0:T(8,128)}), f32[128,256]{1,0:T(8,128)}) %reduce-scatter.20.cloned.1.call-update) | async-done | bytes 131088 | tf_op jit(solution)/shard_map/reduce_scatter | solution.py:43
  353.7 1.0 fusion.13
  354.6 0.1 copy.22
  354.8 16.7 %all_to_all.50 = bf16[8,128,256]{1,2,0:T(8,128)(2,1)S(1)} all-to-all(bf16[8,128,256]{1,2,0:T(8,128)(2,1)S(1)} %stack.24), channel_id=1, replica_groups=mesh['body'=2,'row'=8,'col'=8] {'row'}, dimensions={0} | all-to-all | bytes 1048576 | tf_op jit(solution)/shard_map/all_to_all | solution.py:11
  371.5 7.4 %fusion.30 = f32[128,2048]{1,0:T(8,128)} fusion(bf16[128,2048]{0,1:T(8,128)(2,1)S(1)} %bitcast.124, bf16[2048,2048]{1,0:T(8,128)(2,1)} %bitcast.113), kind=kOutput, calls=%fused_computation.58 | convolution fusion | flops 1073741824 | bytes 9961472 | tf_op jit(solution)/shard_map/dot_general | solution.py:37
  379.0 29.0 %reduce-scatter.22.cloned.1.call-done = f32[128,256]{1,0:T(8,128)} async-done(((f32[128,2048]{1,0:T(8,128)}), f32[128,256]{1,0:T(8,128)}) %reduce-scatter.22.cloned.1.call-update) | async-done | bytes 131088 | tf_op jit(solution)/shard_map/reduce_scatter | solution.py:43
  407.9 1.0 fusion.18
  408.9 0.1 copy.23
  409.1 16.7 %all_to_all.51 = bf16[8,128,256]{1,2,0:T(8,128)(2,1)S(1)} all-to-all(bf16[8,128,256]{1,2,0:T(8,128)(2,1)S(1)} %stack.25), channel_id=1, replica_groups=mesh['body'=2,'row'=8,'col'=8] {'row'}, dimensions={0} | all-to-all | bytes 1048576 | tf_op jit(solution)/shard_map/all_to_all | solution.py:11
  425.8 7.4 %fusion.31 = f32[128,2048]{1,0:T(8,128)} fusion(bf16[128,2048]{0,1:T(8,128)(2,1)S(1)} %bitcast.125, bf16[2048,2048]{1,0:T(8,128)(2,1)} %bitcast.114), kind=kOutput, calls=%fused_computation.59 | convolution fusion | flops 1073741824 | bytes 9961472 | tf_op jit(solution)/shard_map/dot_general | solution.py:37
  433.2 28.9 %reduce-scatter.24.cloned.1.call-done = f32[128,256]{1,0:T(8,128)} async-done(((f32[128,2048]{1,0:T(8,128)}), f32[128,256]{1,0:T(8,128)}) %reduce-scatter.24.cloned.1.call-update) | async-done | bytes 131088 | tf_op jit(solution)/shard_map/reduce_scatter | solution.py:43
  462.1 0.9 fusion.9
  463.1 0.1 copy.24
  463.3 16.7 %all_to_all.52 = bf16[8,128,256]{1,2,0:T(8,128)(2,1)S(1)} all-to-all(bf16[8,128,256]{1,2,0:T(8,128)(2,1)S(1)} %stack.26), channel_id=1, replica_groups=mesh['body'=2,'row'=8,'col'=8] {'row'}, dimensions={0} | all-to-all | bytes 1048576 | tf_op jit(solution)/shard_map/all_to_all | solution.py:11
  479.9 7.4 %fusion.32 = f32[128,2048]{1,0:T(8,128)} fusion(bf16[128,2048]{0,1:T(8,128)(2,1)S(1)} %bitcast.118, bf16[2048,2048]{1,0:T(8,128)(2,1)} %bitcast.115), kind=kOutput, calls=%fused_computation.60 | convolution fusion | flops 1073741824 | bytes 9961472 | tf_op jit(solution)/shard_map/dot_general | solution.py:37
  487.4 28.9 %reduce-scatter.26.cloned.1.call-done = f32[128,256]{1,0:T(8,128)} async-done(((f32[128,2048]{1,0:T(8,128)}), f32[128,256]{1,0:T(8,128)}) %reduce-scatter.26.cloned.1.call-update) | async-done | bytes 131088 | tf_op jit(solution)/shard_map/reduce_scatter | solution.py:43
  516.3 1.7 subtract_bitcast_fusion
  (41 shorter events, 1.0 us)
Async XLA Ops:
  7.2 2.5 copy-start
  7.2 5.5 %collective-permute-start = (f32[128,256]{1,0:T(8,128)}, f32[128,256]{1,0:T(8,128)S(1)}, u32[]{:S(2)}, u32[]{:S(2)}) collective-permute-start(f32[128,256]{1,0:T(8,128)} %bitcast.126), channel_id=1, source_target_pairs={{0,64},{64,0},{1,65},{65,1},{2,66},{66,2},{3,67},{67,3},{4,68},{68... | collective-permute-start | bytes 393224 | tf_op jit(solution)/shard_map/ppermute | solution.py:17
  15.6 17.8 %all-to-all-start = ((bf16[8,128,256]{1,2,0:T(8,128)(2,1)}), bf16[8,128,256]{1,2,0:T(8,128)(2,1)S(1)}, u32[]{:S(2)}, u32[]{:S(2)}) async-start(bf16[8,128,256]{1,2,0:T(8,128)(2,1)} %stack.18), calls=%async_computation | async-start | bytes 1048576 | tf_op jit(solution)/shard_map/all_to_all | solution.py:11
  22.7 53.0 %reduce-scatter.10.cloned.1.call-start = ((), (), s32[]{:S(2)}) async-start(), calls=%async_computation.18 | async-start | bytes 1179648 | tf_op jit(solution)/shard_map/reduce_scatter | solution.py:43
  33.0 7.9 %copy-start.5 = (s32[1,2]{1,0:T(1,128)S(1)}, s32[1,2]{1,0:T(1,128)}, u32[]{:S(2)}) copy-start(s32[1,2]{1,0:T(1,128)} %param.15) | copy-start | bytes 28
  33.0 42.7 %copy-start.1 = (f32[1,128,256]{2,1,0:T(8,128)S(1)}, f32[1,128,256]{2,1,0:T(8,128)}, u32[]{:S(2)}) copy-start(f32[1,128,256]{2,1,0:T(8,128)} %param.11) | copy-start | bytes 393220
  40.8 89.2 %reduce-scatter.12.cloned.1.call-start = ((), (), s32[]{:S(2)}) async-start(), calls=%async_computation.19 | async-start | bytes 1179648 | tf_op jit(solution)/shard_map/reduce_scatter | solution.py:43
  75.7 54.3 %copy-start.3 = (f32[128,256]{1,0:T(8,128)S(1)}, f32[128,256]{1,0:T(8,128)}, u32[]{:S(2)}) copy-start(f32[128,256]{1,0:T(8,128)} %reduce-scatter.10.cloned.1.call-done) | copy-start | bytes 393220
  101.1 83.2 %reduce-scatter.14.cloned.1.call-start = ((), (), s32[]{:S(2)}) async-start(), calls=%async_computation.20 | async-start | bytes 1179648 | tf_op jit(solution)/shard_map/reduce_scatter | solution.py:43
  155.3 83.2 %copy-start.2 = (f32[1,128,256]{2,1,0:T(8,128)S(1)}, f32[1,128,256]{2,1,0:T(8,128)}, u32[]{:S(2)}) copy-start(f32[1,128,256]{2,1,0:T(8,128)} %param.10) | copy-start | bytes 393220
  155.3 83.2 %reduce-scatter.16.cloned.1.call-start = ((), (), s32[]{:S(2)}) async-start(), calls=%async_computation.21 | async-start | bytes 1179648 | tf_op jit(solution)/shard_map/reduce_scatter | solution.py:43
  209.5 89.8 %reduce-scatter.18.cloned.1.call-start = ((), (), s32[]{:S(2)}) async-start(), calls=%async_computation.22 | async-start | bytes 1179648 | tf_op jit(solution)/shard_map/reduce_scatter | solution.py:43
  239.5 5.0 collective-permute-start.1
  269.9 83.8 %reduce-scatter.20.cloned.1.call-start = ((), (), s32[]{:S(2)}) async-start(), calls=%async_computation.23 | async-start | bytes 1179648 | tf_op jit(solution)/shard_map/reduce_scatter | solution.py:43
  299.3 54.3 %copy-start.4 = (f32[128,256]{1,0:T(8,128)S(1)}, f32[128,256]{1,0:T(8,128)}, u32[]{:S(2)}) copy-start(f32[128,256]{1,0:T(8,128)} %reduce-scatter.18.cloned.1.call-done) | copy-start | bytes 393220
  324.8 83.2 %reduce-scatter.22.cloned.1.call-start = ((), (), s32[]{:S(2)}) async-start(), calls=%async_computation.24 | async-start | bytes 1179648 | tf_op jit(solution)/shard_map/reduce_scatter | solution.py:43
  378.9 83.2 %reduce-scatter.24.cloned.1.call-start = ((), (), s32[]{:S(2)}) async-start(), calls=%async_computation.25 | async-start | bytes 1179648 | tf_op jit(solution)/shard_map/reduce_scatter | solution.py:43
  433.2 83.1 %reduce-scatter.26.cloned.1.call-start = ((), (), s32[]{:S(2)}) async-start(), calls=%async_computation.26 | async-start | bytes 1179648 | tf_op jit(solution)/shard_map/reduce_scatter | solution.py:43
Sparse Core Ops, SparseCore 0:
  41.0 34.6 reduce-scatter.9
  101.2 28.7 reduce-scatter.11
  155.5 28.7 reduce-scatter.13
  209.7 28.8 reduce-scatter.15
  270.0 29.2 reduce-scatter.17
  324.9 28.7 reduce-scatter.19
  379.0 28.8 reduce-scatter.21
  433.3 28.7 reduce-scatter.23
  487.5 28.7 reduce-scatter.25
